TPU v7x, 32 devices: a whole 2x2x4 slice. The times are simulated.
32 devices in a mesh: isl: 4 (over x, core), fsdp: 8 (over z, y).
Axes of the slice: x: 2, y: 2, z: 4, core: 2. Of those that a mesh axis runs over, the one named last changes fastest.
Arguments:
- weights: float32 [3, 7168, 4096], P(None, 'fsdp', 'isl'), may hold values from -6 to 6
- momentum: float32 [3, 7168, 4096], P(None, 'fsdp', 'isl'), may hold values from -0.12 to 0.12
- first_moment: bfloat16 [4, 3, 7168, 4096], P('isl', None, 'fsdp'), may hold values from -0.00029945374 to 0.00029945374
- second_moment: bfloat16 [4, 3, 7168, 4096], P('isl', None, 'fsdp'), may hold values from 9.95351e-09 to 9.953976e-06
- inputs: bfloat16 [2, 256, 4096], P(None, ('isl', 'fsdp')), may hold values from -6 to 6
- targets: bfloat16 [2, 256, 4096], P(None, ('isl', 'fsdp')), may hold values from -6 to 6
- overflow_step: int32 [4, 8], P('isl', 'fsdp'), may hold values from 0 to 15
Outputs:
- new_weights: float32 [3, 7168, 4096], P(None, 'fsdp', 'isl')
- new_momentum: float32 [3, 7168, 4096], P(None, 'fsdp', 'isl')
Inputs may be any that keep to these rules, and one draw needn't show every extreme that they name: `overflow_step`: A device reports an overflow at inner step k when its value equals k; values of 2 or more report none.
All inputs are finite; a program needn't handle non-finite values.
Results may differ from a plain program's by a relative error of at most 0.004.
Values may be sent and summed in bfloat16 or wider, within the bound.
A program may use at most 320 MiB of HBM per device.

v0:
```python
import math
import jax
import jax.numpy as jnp
from jax import lax
from jax.sharding import PartitionSpec as P

D = 4096
FF = 7168
inner_rate = 0.02
beta_first = 0.9
beta_second = 0.95
epsilon = 1e-08
decay_rate = 0.1
outer_rate = 0.7
nesterov_coef = 0.9


def silu_parts(preact):
    sigmoid_value = jax.nn.sigmoid(preact)
    return (preact * sigmoid_value, sigmoid_value * (1.0 + preact * (1.0 - sigmoid_value)))


def contract_last(left_side, right_side):
    return lax.dot_general(
        left_side, right_side, (((1,), (1,)), ((), ())), preferred_element_type=jnp.float32
    )


def contract_first(left_side, right_side):
    return lax.dot_general(
        left_side, right_side, (((0,), (0,)), ((), ())), preferred_element_type=jnp.float32
    )


def body(weights, momentum, first_moment, second_moment, inputs, targets, overflow_step):
    island_count = lax.axis_size("isl")
    gathered = lax.all_gather(weights.astype(jnp.bfloat16), "isl", axis=2, tiled=True).astype(
        weights.dtype
    )
    current = gathered
    moment_one = first_moment[0].astype(jnp.float32)
    moment_two = second_moment[0].astype(jnp.float32)
    inner_count = inputs.shape[0]
    island_tokens = inputs.shape[1] * lax.axis_size("fsdp")
    for inner_step in range(inner_count):
        rounded = current.astype(jnp.bfloat16)
        local_inputs = inputs[inner_step]
        local_targets = targets[inner_step]
        every_input = lax.all_gather(local_inputs, "fsdp", axis=0, tiled=True)
        gate_pre = contract_last(every_input, rounded[0]) / math.sqrt(D)
        up_pre = contract_last(every_input, rounded[1]) / math.sqrt(D)
        activated, slope = silu_parts(gate_pre)
        hidden = (activated * up_pre).astype(jnp.bfloat16)
        partial_value = jnp.dot(hidden, rounded[2], preferred_element_type=jnp.float32)
        summed = lax.psum_scatter(partial_value, "fsdp", scatter_dimension=0, tiled=True)
        outputs = local_inputs.astype(jnp.float32) + summed / math.sqrt(FF)
        own_slopes = ((outputs - local_targets.astype(jnp.float32)) / island_tokens).astype(
            jnp.bfloat16
        )
        slopes = lax.all_gather(own_slopes, "fsdp", axis=0, tiled=True)
        hidden_slope = contract_last(slopes, rounded[2]) / math.sqrt(FF)
        gate_slope = (hidden_slope * up_pre * slope).astype(jnp.bfloat16)
        up_slope = (hidden_slope * activated).astype(jnp.bfloat16)
        grad_gate = contract_first(gate_slope, every_input) / math.sqrt(D)
        grad_up = contract_first(up_slope, every_input) / math.sqrt(D)
        grad_down = contract_first(hidden, slopes) / math.sqrt(FF)
        gradient = jnp.stack([grad_gate, grad_up, grad_down])
        overflow_count = lax.psum(jnp.sum((overflow_step == inner_step).astype(jnp.int32)), "fsdp")
        skipped = overflow_count > 0
        next_one = beta_first * moment_one + (1.0 - beta_first) * gradient
        next_two = beta_second * moment_two + (1.0 - beta_second) * gradient * gradient
        next_weights = current - inner_rate * (
            next_one / (jnp.sqrt(next_two) + epsilon) + decay_rate * current
        )
        current = jnp.where(skipped, current, next_weights)
        moment_one = jnp.where(skipped, moment_one, next_one)
        moment_two = jnp.where(skipped, moment_two, next_two)
    pseudo_term = gathered - current
    pseudo_sum = lax.psum_scatter(
        pseudo_term.astype(jnp.bfloat16), "isl", scatter_dimension=2, tiled=True
    ).astype(jnp.float32)
    outer_delta = pseudo_sum / island_count
    new_momentum = nesterov_coef * momentum + outer_delta
    new_weights = weights - outer_rate * (outer_delta + nesterov_coef * new_momentum)
    return (new_weights, new_momentum)


def solution(mesh):
    in_specs = (
        P(None, "fsdp", "isl"),
        P(None, "fsdp", "isl"),
        P("isl", None, "fsdp", None),
        P("isl", None, "fsdp", None),
        P(None, ("isl", "fsdp"), None),
        P(None, ("isl", "fsdp"), None),
        P("isl", "fsdp"),
    )
    out_specs = (P(None, "fsdp", "isl"), P(None, "fsdp", "isl"))
    return jax.shard_map(body, mesh=mesh, in_specs=in_specs, out_specs=out_specs, check_vma=False)
```

profile of v0, /device:TPU:0, one launch (start us, length us, event | category | flops | bytes accessed | tf_op | source)
XLA Modules:
  0.0 742.3 jit_solution(11448061210267699757)
XLA Ops:
  7.2 0.0 copy-start.1
  7.2 0.0 copy-start.2
  7.2 0.0 all-gather.4.cloned.1.call-start
  7.2 7.5 %convert_element_type.72 = bf16[3,896,1024]{2,1,0:T(8,128)(2,1)} convert(f32[3,896,1024]{2,1,0:T(8,128)} %param.7) | non-fusion elementwise | flops 2752512 | bytes 16515072 | tf_op jit(solution)/shard_map/convert_element_type | solution.py:37
  14.7 0.0 all-gather.4.cloned.1.call-update
  14.8 0.0 reduce-scatter.4.cloned.1.call-start
  14.8 0.0 copy-done.1
  14.8 33.0 %all-gather = bf16[1,64,4096]{2,1,0:T(8,128)(2,1)S(1)} all-gather(bf16[1,8,4096]{2,1,0:T(8,128)(2,1)S(1)} %get-tuple-element.7), channel_id=2, replica_groups=mesh['isl'=4,'fsdp'=8] {'fsdp'}, dimensions={1}, use_global_device_ids=true | all-gather | bytes 589824 | tf_op jit(solution)/shard_map/all_gather | solution.py:49
  47.9 107.2 %all-gather.4.cloned.1.call-done = bf16[3,896,4096]{2,1,0:T(8,128)(2,1)} async-done(((bf16[3,896,1024]{2,1,0:T(8,128)(2,1)}), bf16[3,896,4096]{2,1,0:T(8,128)(2,1)}) %all-gather.4.cloned.1.call-update) | async-done | bytes 22020112 | tf_op jit(solution)/shard_map/all_gather | solution.py:37
  155.0 5.4 fusion.24
  160.5 5.4 multiply_convert_fusion.5
  165.9 5.5 fusion.19
  171.4 0.0 reduce-scatter.4.cloned.1.call-update
  171.4 0.0 reduce-scatter.6.cloned.1.call-start
  172.1 13.0 %all-reduce = (s32[]{:T(128)}, s32[]{:T(128)}) all-reduce(s32[]{:T(128)} %bitcast.1, s32[]{:T(128)} %bitcast), channel_id=1, replica_groups=mesh['isl'=4,'fsdp'=8] {'fsdp'}, use_global_device_ids=true, to_apply=%region_1.0 | all-reduce | flops 2 | bytes 16 | tf_op jit(solution)/shard_map/psum | solution.py:68
  185.8 31.7 %all-gather.1 = bf16[1,64,4096]{2,1,0:T(8,128)(2,1)S(1)} all-gather(bf16[1,8,4096]{2,1,0:T(8,128)(2,1)S(1)} %get-tuple-element.6), channel_id=3, replica_groups=mesh['isl'=4,'fsdp'=8] {'fsdp'}, dimensions={1}, use_global_device_ids=true | all-gather | bytes 589824 | tf_op jit(solution)/shard_map/all_gather | solution.py:49
  217.4 18.9 %reduce-scatter.4.cloned.1.call-done = f32[8,4096]{1,0:T(8,128)} async-done(((f32[64,4096]{1,0:T(8,128)}), f32[8,4096]{1,0:T(8,128)}) %reduce-scatter.4.cloned.1.call-update) | async-done | bytes 131088 | tf_op jit(solution)/shard_map/reduce_scatter | solution.py:55
  236.4 0.0 copy-done.2
  236.4 0.9 fusion.43
  237.3 31.7 %all_gather.17 = bf16[64,4096]{1,0:T(8,128)(2,1)S(1)} all-gather(bf16[8,4096]{1,0:T(8,128)(2,1)S(1)} %fusion.43), channel_id=1, replica_groups=mesh['isl'=4,'fsdp'=8] {'fsdp'}, dimensions={0}, use_global_device_ids=true | all-gather | bytes 589824 | tf_op jit(solution)/shard_map/all_gather | solution.py:60
  268.9 2.1 multiply_bitcast_fusion.3
  271.0 0.0 copy-start
  271.1 10.6 %fusion.23 = f32[64,896]{1,0:T(8,128)S(1)} fusion(bf16[64,4096]{1,0:T(8,128)(2,1)S(1)} %all_gather.17, bf16[3,896,4096]{2,1,0:T(8,128)(2,1)} %all-gather.4.cloned.1.call-done), kind=kOutput, calls=%fused_computation.51 | convolution fusion | flops 469819392 | bytes 8093696 | tf_op jit(solution)/shard_map/dot_general | solution.py:24
  281.7 7.2 multiply_bitcast_fusion.4
  288.9 7.3 multiply_bitcast_fusion.5
  296.2 47.5 %fusion.52 = bf16[3,896,4096]{2,1,0:T(8,128)(2,1)} fusion(bf16[1,3,896,4096]{3,2,1,0:T(8,128)(2,1)} %param.10, f32[1,896,4096]{2,1,0:T(8,128)S(1)} %multiply_bitcast_fusion.3, f32[1,896,4096]{2,1,0:T(8,128)} %multiply_bitcast_fusion.4, f32[1,896,4096]{2,1,0:T(8,128)} %multiply_bitcast_fusion.5, bf16[1,3,896,4096]{3,2,1,0:T(8,128)(2,1)} %param.9, ...), kind=kLoop, calls=%fused_computation.90 | loop fusion | flops 220200960 | bytes 132120576 | tf_op jit(solution)/shard_map/convert_element_type | solution.py:46
  343.8 0.0 copy-done
  343.8 5.4 fusion.27
  349.2 5.4 multiply_convert_fusion.2
  354.7 5.5 fusion.21
  360.1 0.0 reduce-scatter.6.cloned.1.call-update
  360.1 0.0 reduce-scatter.8.cloned.1.call-start
  360.7 62.5 %reduce-scatter.6.cloned.1.call-done = f32[8,4096]{1,0:T(8,128)} async-done(((f32[64,4096]{1,0:T(8,128)}), f32[8,4096]{1,0:T(8,128)}) %reduce-scatter.6.cloned.1.call-update) | async-done | bytes 131088 | tf_op jit(solution)/shard_map/reduce_scatter | solution.py:55
  423.2 0.9 fusion.41
  424.2 31.7 %all_gather.19 = bf16[64,4096]{1,0:T(8,128)(2,1)S(1)} all-gather(bf16[8,4096]{1,0:T(8,128)(2,1)S(1)} %fusion.41), channel_id=1, replica_groups=mesh['isl'=4,'fsdp'=8] {'fsdp'}, dimensions={0}, use_global_device_ids=true | all-gather | bytes 589824 | tf_op jit(solution)/shard_map/all_gather | solution.py:60
  455.9 5.4 fusion.22
  461.3 7.3 multiply_bitcast_fusion
  468.6 7.2 multiply_bitcast_fusion.1
  475.8 7.3 multiply_bitcast_fusion.2
  483.1 77.6 %fusion.13 = bf16[3,896,4096]{2,1,0:T(8,128)(2,1)} fusion(bf16[3,896,4096]{2,1,0:T(8,128)(2,1)} %all-gather.4.cloned.1.call-done, f32[1,896,4096]{2,1,0:T(8,128)} %multiply_bitcast_fusion, f32[1,896,4096]{2,1,0:T(8,128)} %multiply_bitcast_fusion.1, f32[1,896,4096]{2,1,0:T(8,128)} %multiply_bitcast_fusion.2, f32[1,896,4096]{2,1,0:T(8,128)} %copy-done, ...), kind=kLoop, calls=%fused_computation.24 | loop fusion | flops 429391872 | bytes 176160768 | tf_op jit(solution)/shard_map/convert_element_type | solution.py:80
  560.7 0.0 reduce-scatter.8.cloned.1.call-update
  560.7 155.7 %reduce-scatter.8.cloned.1.call-done = bf16[3,896,1024]{2,1,0:T(8,128)(2,1)} async-done(((bf16[3,896,4096]{2,1,0:T(8,128)(2,1)}), bf16[3,896,1024]{2,1,0:T(8,128)(2,1)}) %reduce-scatter.8.cloned.1.call-update) | async-done | bytes 5505040 | tf_op jit(solution)/shard_map/reduce_scatter | solution.py:79
  716.4 19.4 %multiply_subtract_fusion = (f32[3,896,1024]{2,1,0:T(8,128)}, f32[3,896,1024]{2,1,0:T(8,128)}) fusion(f32[3,896,1024]{2,1,0:T(8,128)} %param.7, bf16[3,896,1024]{2,1,0:T(8,128)(2,1)} %reduce-scatter.8.cloned.1.call-done, f32[3,896,1024]{2,1,0:T(8,128)} %param.8), kind=kLoop, calls=%fused_computation.33 | loop fusion | flops 22020096 | bytes 49545216 | tf_op jit(solution)/shard_map/sub | solution.py:84
  (1 shorter events, 0.0 us)
Async XLA Ops:
  7.2 7.7 %copy-start.1 = (bf16[2,8,4096]{2,1,0:T(8,128)(2,1)S(1)}, bf16[2,8,4096]{2,1,0:T(8,128)(2,1)}, u32[]{:S(2)}) copy-start(bf16[2,8,4096]{2,1,0:T(8,128)(2,1)} %param.11) | copy-start | bytes 393220
  7.2 229.2 %copy-start.2 = (bf16[2,8,4096]{2,1,0:T(8,128)(2,1)S(1)}, bf16[2,8,4096]{2,1,0:T(8,128)(2,1)}, u32[]{:S(2)}) copy-start(bf16[2,8,4096]{2,1,0:T(8,128)(2,1)} %param.12) | copy-start | bytes 393220
  7.2 147.8 %all-gather.4.cloned.1.call-start = ((), (), s32[]{:S(2)}) async-start(), calls=%async_computation.3 | async-start | bytes 27525120 | tf_op jit(solution)/shard_map/all_gather | solution.py:37
  14.8 221.6 %reduce-scatter.4.cloned.1.call-start = ((), (), s32[]{:S(2)}) async-start(), calls=%async_computation.4 | async-start | bytes 1179648 | tf_op jit(solution)/shard_map/reduce_scatter | solution.py:55
  171.4 251.8 %reduce-scatter.6.cloned.1.call-start = ((), (), s32[]{:S(2)}) async-start(), calls=%async_computation.5 | async-start | bytes 1179648 | tf_op jit(solution)/shard_map/reduce_scatter | solution.py:55
  271.0 72.7 %copy-start = (f32[1,896,4096]{2,1,0:T(8,128)}, f32[1,896,4096]{2,1,0:T(8,128)S(1)}, u32[]{:S(2)}) copy-start(f32[1,896,4096]{2,1,0:T(8,128)S(1)} %multiply_bitcast_fusion.3) | copy-start | bytes 44040196
  360.1 356.3 %reduce-scatter.8.cloned.1.call-start = ((), (), s32[]{:S(2)}) async-start(), calls=%async_computation.6 | async-start | bytes 27525120 | tf_op jit(solution)/shard_map/reduce_scatter | solution.py:79
Sparse Core Ops, SparseCore 0:
  14.9 140.0 all-gather.3
  171.5 64.7 reduce-scatter.3
  360.3 62.9 reduce-scatter.5
  560.8 155.5 reduce-scatter.7
where the time goes:
time: 743 us; the launch traced here: 742 us
  waiting for transfers between devices  344 us (46%)
  other arithmetic  154 us (21%)
  blocking collectives  141 us (19%)
  matrix products  87.2 us (12%)
  between operations  15.7 us (2%)
    reduce_scatter x1, waiting for transfers between devices, body(): lax.psum_scatter(pseudo_term.astype(jnp.bfloat16), 'isl', scatter_dimensi...  156 us
    all_gather x1, waiting for transfers between devices, body(): lax.all_gather(weights.astype(jnp.bfloat16), 'isl', axis=2, tiled=True)  107 us
    reduce_scatter x2, waiting for transfers between devices, body(): lax.psum_scatter(partial_value, 'fsdp', scatter_dimension=0, tiled=True)  81.4 us
    convert_element_type x1, other arithmetic, body(): pseudo_term.astype(jnp.bfloat16)  77.6 us
    all_gather x2, blocking collectives, body(): every_input = lax.all_gather(local_inputs, 'fsdp', axis=0, tiled=True)  64.7 us
    all_gather x2, blocking collectives, body(): slopes = lax.all_gather(own_slopes, 'fsdp', axis=0, tiled=True)  63.4 us
    convert_element_type x1, other arithmetic, body(): rounded = current.astype(jnp.bfloat16)  47.5 us
    dot_general x6, matrix products, contract_first(): lax.dot_general(left_side, right_side, (((0,), (0,)), ((), ())), preferre...  38.4 us
  transfers between devices with their start and end apart: 4, of which 4 were waited for; matrix products, arithmetic and copies ran while one was open for 0% of the time, Pallas kernels for 0%

commit v1 on v0

--- a/solution.py
+++ b/solution.py
@@ -34,7 +34,7 @@
 
 def body(weights, momentum, first_moment, second_moment, inputs, targets, overflow_step):
     island_count = lax.axis_size("isl")
-    gathered = lax.all_gather(weights.astype(jnp.bfloat16), "isl", axis=2, tiled=True).astype(
+    gathered = jnp.concatenate(lax.all_gather(weights.astype(jnp.bfloat16), "isl"), axis=2).astype(
         weights.dtype
     )
     current = gathered

time: 743 us -> 859 us (1.16)
  local copies, waits for them, and re-layouts: 0.02 us -> 103 us
  other arithmetic: 154 us -> 189 us
  waiting for transfers between devices: 344 us -> 325 us
    convert_element_type x0 -> x1, local copies, waits for them, and re-layouts: none -> 51.9 us  [body(): jnp.concatenate(lax.all_gather(weights.astype(jnp.bfloat16), 'isl'), axis=2)]
    unnamed x6 -> x11, local copies, waits for them, and re-layouts: 0.01 us -> 32.6 us
    reshape x0 -> x1, other arithmetic: none -> 30.7 us  [body(): jnp.concatenate(lax.all_gather(weights.astype(jnp.bfloat16), 'isl'), axis=2)]
    reduce_scatter x2, waiting for transfers between devices: 81.4 us -> 61.8 us  [body(): lax.psum_scatter(partial_value, 'fsdp', scatter_dimension=0, tiled=True)]
    slice x0 -> x1, local copies, waits for them, and re-layouts: none -> 18.8 us  [body(): rounded[2]]
  transfers between devices with their start and end apart: 4 -> 4, of which waited for: 4 -> 3; matrix products, arithmetic and copies ran while one was open for 0% -> 6% of each run, Pallas kernels for 0% -> 0%
where the time goes in v1:
time: 859 us; the launch traced here: 854 us
  waiting for transfers between devices  325 us (38%)
  other arithmetic  189 us (22%)
  blocking collectives  141 us (16%)
  local copies, waits for them, and re-layouts  103 us (12%)
  matrix products  79.5 us (9%)
  between operations  16.1 us (2%)
    reduce_scatter x1, waiting for transfers between devices, body(): lax.psum_scatter(pseudo_term.astype(jnp.bfloat16), 'isl', scatter_dimensi...  156 us
    all_gather x1, waiting for transfers between devices, body(): lax.all_gather(weights.astype(jnp.bfloat16), 'isl')  107 us
    convert_element_type x1, other arithmetic, body(): pseudo_term.astype(jnp.bfloat16)  76.8 us
    all_gather x2, blocking collectives, body(): every_input = lax.all_gather(local_inputs, 'fsdp', axis=0, tiled=True)  64.6 us
    all_gather x2, blocking collectives, body(): slopes = lax.all_gather(own_slopes, 'fsdp', axis=0, tiled=True)  63.3 us
    reduce_scatter x2, waiting for transfers between devices, body(): lax.psum_scatter(partial_value, 'fsdp', scatter_dimension=0, tiled=True)  61.8 us
    convert_element_type x1, other arithmetic, body(): rounded = current.astype(jnp.bfloat16)  52.6 us
    convert_element_type x1, local copies, waits for them, and re-layouts, body(): jnp.concatenate(lax.all_gather(weights.astype(jnp.bfloat16), 'isl'), axis=2)  51.9 us
  transfers between devices with their start and end apart: 4, of which 3 were waited for; matrix products, arithmetic and copies ran while one was open for 6% of the time, Pallas kernels for 0%

profile of v1, /device:TPU:0, one launch (start us, length us, event | category | flops | bytes accessed | tf_op | source)
XLA Modules:
  0.0 853.5 jit_solution(12643583377808924011)
XLA Ops:
  7.2 0.0 copy-start.2
  7.2 0.0 all-gather.5.cloned.1.call-start
  7.2 7.5 convert_element_type.75
  14.7 0.0 all-gather.5.cloned.1.call-update
  14.7 0.0 reduce-scatter.4.cloned.1.call-start
  14.8 0.0 copy-done.2
  14.8 33.0 %all-gather.1 = bf16[1,64,4096]{2,1,0:T(8,128)(2,1)S(1)} all-gather(bf16[1,8,4096]{2,1,0:T(8,128)(2,1)S(1)} %get-tuple-element.12), channel_id=3, replica_groups=mesh['isl'=4,'fsdp'=8] {'fsdp'}, dimensions={1}, use_global_device_ids=true | all-gather | bytes 589824 | tf_op jit(solution)/shard_map/all_gather | solution.py:49
  47.8 107.2 %all-gather.5.cloned.1.call-done = bf16[12,896,1024]{2,1,0:T(8,128)(2,1)} async-done(((bf16[3,896,1024]{2,1,0:T(8,128)(2,1)}), bf16[12,896,1024]{2,1,0:T(8,128)(2,1)}) %all-gather.5.cloned.1.call-update) | async-done | bytes 22020112 | tf_op jit(solution)/shard_map/all_gather | solution.py:37
  155.0 30.7 %copy_bitcast_fusion = (bf16[3,896,4,1024]{3,2,1,0:T(4,128)(2,1)}, f32[3,896,4,1024]{3,2,1,0:T(4,128)}) fusion(bf16[4,3,896,1024]{3,2,1,0:T(8,128)(2,1)} %bitcast.123), kind=kLoop, calls=%fused_computation.23 | loop fusion | flops 11010048 | bytes 88080384 | tf_op jit(solution)/shard_map/reshape | solution.py:37
  185.7 18.8 %fusion.46 = (bf16[1,896,4,1024]{3,2,1,0:T(4,128)(2,1)}, bf16[1,896,4,1024]{3,2,1,0:T(4,128)(2,1)}, bf16[1,896,4,1024]{3,2,1,0:T(4,128)(2,1)}) fusion(bf16[3,896,4,1024]{3,2,1,0:T(4,128)(2,1)} %get-tuple-element.9), kind=kLoop, calls=%fused_computation.82 | loop fusion | bytes 44040192 | tf_op jit(solution)/shard_map/slice | solution.py:54
  204.5 7.9 copy.13
  212.4 0.0 copy-start.1
  212.4 13.5 %copy.12 = bf16[112,8,4,1024]{3,1,2,0:T(8,128)(2,1)} copy(bf16[112,8,4,1024]{3,2,1,0:T(4,128)(2,1)} %bitcast.121) | data formatting | bytes 14680064
  225.9 11.1 %copy.11 = bf16[112,8,4,1024]{3,1,2,0:T(8,128)(2,1)} copy(bf16[112,8,4,1024]{3,2,1,0:T(4,128)(2,1)} %bitcast.120) | data formatting | bytes 14680064
  237.0 5.4 convolution_multiply_fusion.2
  242.5 5.4 multiply_convert_fusion.5
  247.9 0.0 copy-done.1
  247.9 2.4 fusion.48
  250.3 0.0 reduce-scatter.4.cloned.1.call-update
  250.3 0.0 reduce-scatter.6.cloned.1.call-start
  251.0 13.1 %all-reduce = (s32[]{:T(128)}, s32[]{:T(128)}) all-reduce(s32[]{:T(128)} %bitcast.3, s32[]{:T(128)} %bitcast.2), channel_id=1, replica_groups=mesh['isl'=4,'fsdp'=8] {'fsdp'}, use_global_device_ids=true, to_apply=%region_1.0 | all-reduce | flops 2 | bytes 16 | tf_op jit(solution)/shard_map/psum | solution.py:68
  264.8 31.6 %all-gather.2 = bf16[1,64,4096]{2,1,0:T(8,128)(2,1)S(1)} all-gather(bf16[1,8,4096]{2,1,0:T(8,128)(2,1)S(1)} %get-tuple-element.11), channel_id=4, replica_groups=mesh['isl'=4,'fsdp'=8] {'fsdp'}, dimensions={1}, use_global_device_ids=true | all-gather | bytes 589824 | tf_op jit(solution)/shard_map/all_gather | solution.py:49
  296.3 51.9 %reshape.29 = f32[3,896,4096]{2,1,0:T(8,128)} reshape(f32[3,896,4,1024]{3,2,1,0:T(4,128)} %get-tuple-element.10) | data formatting | bytes 88080384 | tf_op jit(solution)/shard_map/convert_element_type | solution.py:37
  348.3 0.0 copy-done.3
  348.3 0.9 fusion.35
  349.2 31.6 %all_gather.21 = bf16[64,4096]{1,0:T(8,128)(2,1)S(1)} all-gather(bf16[8,4096]{1,0:T(8,128)(2,1)S(1)} %fusion.35), channel_id=1, replica_groups=mesh['isl'=4,'fsdp'=8] {'fsdp'}, dimensions={0}, use_global_device_ids=true | all-gather | bytes 589824 | tf_op jit(solution)/shard_map/all_gather | solution.py:60
  380.8 5.4 convolution_multiply_fusion
  386.3 2.1 multiply_bitcast_fusion.3
  388.4 0.0 copy-start
  388.4 7.9 multiply_bitcast_fusion.4
  396.3 7.3 multiply_bitcast_fusion.5
  403.6 52.6 %fusion.45 = bf16[3,896,4096]{2,1,0:T(8,128)(2,1)} fusion(f32[3,896,4096]{2,1,0:T(8,128)} %reshape.29, bf16[1,3,896,4096]{3,2,1,0:T(8,128)(2,1)} %param.10, f32[1,896,4096]{2,1,0:T(8,128)S(1)} %multiply_bitcast_fusion.3, f32[1,896,4096]{2,1,0:T(8,128)} %multiply_bitcast_fusion.4, f32[1,896,4096]{2,1,0:T(8,128)} %multiply_bitcast_fusion.5, ...), kind=kLoop, calls=%fused_computation.81 | loop fusion | flops 209190912 | bytes 154140672 | tf_op jit(solution)/shard_map/convert_element_type | solution.py:46
  456.2 5.4 fusion.19
  461.6 5.4 multiply_convert_fusion.2
  467.1 5.5 fusion.16
  472.5 0.0 reduce-scatter.6.cloned.1.call-update
  472.6 0.0 reduce-scatter.8.cloned.1.call-start
  473.3 61.8 %reduce-scatter.6.cloned.1.call-done = f32[8,4096]{1,0:T(8,128)} async-done(((f32[64,4096]{1,0:T(8,128)}), f32[8,4096]{1,0:T(8,128)}) %reduce-scatter.6.cloned.1.call-update) | async-done | bytes 131088 | tf_op jit(solution)/shard_map/reduce_scatter | solution.py:55
  535.1 0.9 fusion.33
  536.0 31.7 %all_gather.23 = bf16[64,4096]{1,0:T(8,128)(2,1)S(1)} all-gather(bf16[8,4096]{1,0:T(8,128)(2,1)S(1)} %fusion.33), channel_id=1, replica_groups=mesh['isl'=4,'fsdp'=8] {'fsdp'}, dimensions={0}, use_global_device_ids=true | all-gather | bytes 589824 | tf_op jit(solution)/shard_map/all_gather | solution.py:60
  567.7 5.4 fusion.17
  573.2 7.2 multiply_bitcast_fusion
  580.4 7.2 multiply_bitcast_fusion.1
  587.6 7.3 multiply_bitcast_fusion.2
  594.9 76.8 %fusion.12 = bf16[3,896,4096]{2,1,0:T(8,128)(2,1)} fusion(f32[3,896,4096]{2,1,0:T(8,128)} %reshape.29, f32[1,896,4096]{2,1,0:T(8,128)} %multiply_bitcast_fusion, f32[1,896,4096]{2,1,0:T(8,128)} %multiply_bitcast_fusion.1, f32[1,896,4096]{2,1,0:T(8,128)} %multiply_bitcast_fusion.2, f32[1,896,4096]{2,1,0:T(8,128)} %copy-done, ...), kind=kLoop, calls=%fused_computation.22 | loop fusion | flops 418381824 | bytes 198180864 | tf_op jit(solution)/shard_map/convert_element_type | solution.py:80
  671.7 0.0 reduce-scatter.8.cloned.1.call-update
  671.7 155.7 %reduce-scatter.8.cloned.1.call-done = bf16[3,896,1024]{2,1,0:T(8,128)(2,1)} async-done(((bf16[3,896,4096]{2,1,0:T(8,128)(2,1)}), bf16[3,896,1024]{2,1,0:T(8,128)(2,1)}) %reduce-scatter.8.cloned.1.call-update) | async-done | bytes 5505040 | tf_op jit(solution)/shard_map/reduce_scatter | solution.py:79
  827.4 19.4 %multiply_subtract_fusion = (f32[3,896,1024]{2,1,0:T(8,128)}, f32[3,896,1024]{2,1,0:T(8,128)}) fusion(f32[3,896,1024]{2,1,0:T(8,128)} %param.7, bf16[3,896,1024]{2,1,0:T(8,128)(2,1)} %reduce-scatter.8.cloned.1.call-done, f32[3,896,1024]{2,1,0:T(8,128)} %param.8), kind=kLoop, calls=%fused_computation.30 | loop fusion | flops 22020096 | bytes 49545216 | tf_op jit(solution)/shard_map/sub | solution.py:84
  (4 shorter events, 0.0 us)
Async XLA Ops:
  7.2 7.6 copy-start.2
  7.2 147.8 %all-gather.5.cloned.1.call-start = ((), (), s32[]{:S(2)}) async-start(), calls=%async_computation.6 | async-start | bytes 27525120 | tf_op jit(solution)/shard_map/all_gather | solution.py:37
  14.7 333.6 %reduce-scatter.4.cloned.1.call-start = ((), (), s32[]{:S(2)}) async-start(), calls=%async_computation.3 | async-start | bytes 1179648 | tf_op jit(solution)/shard_map/reduce_scatter | solution.py:55
  212.4 35.5 %copy-start.1 = (bf16[112,8,4,1024]{3,1,2,0:T(8,128)(2,1)}, bf16[112,8,4,1024]{3,1,2,0:T(8,128)(2,1)S(1)}, u32[]{:S(2)}) copy-start(bf16[112,8,4,1024]{3,1,2,0:T(8,128)(2,1)S(1)} %copy.13) | copy-start | bytes 22020100
  250.3 284.7 %reduce-scatter.6.cloned.1.call-start = ((), (), s32[]{:S(2)}) async-start(), calls=%async_computation.4 | async-start | bytes 1179648 | tf_op jit(solution)/shard_map/reduce_scatter | solution.py:55
  296.3 51.9 %copy-start.3 = (bf16[2,8,4096]{2,1,0:T(8,128)(2,1)S(1)}, bf16[2,8,4096]{2,1,0:T(8,128)(2,1)}, u32[]{:S(2)}) copy-start(bf16[2,8,4096]{2,1,0:T(8,128)(2,1)} %param.12) | copy-start | bytes 393220
  388.4 67.9 %copy-start = (f32[1,896,4096]{2,1,0:T(8,128)}, f32[1,896,4096]{2,1,0:T(8,128)S(1)}, u32[]{:S(2)}) copy-start(f32[1,896,4096]{2,1,0:T(8,128)S(1)} %multiply_bitcast_fusion.3) | copy-start | bytes 44040196
  472.6 354.8 %reduce-scatter.8.cloned.1.call-start = ((), (), s32[]{:S(2)}) async-start(), calls=%async_computation.5 | async-start | bytes 27525120 | tf_op jit(solution)/shard_map/reduce_scatter | solution.py:79
Sparse Core Ops, SparseCore 0:
  14.8 140.0 all-gather.4
  250.5 64.6 reduce-scatter.3
  472.7 62.3 reduce-scatter.5
  671.8 155.4 reduce-scatter.7
